TPU v7x, 32 devices: a whole 2x2x4 slice. The times are simulated.
32 devices in a mesh: groups: 2 (over y), epoch: 4 (over z), space: 2 (over x), sub: 2 (over core).
Axes of the slice: x: 2, y: 2, z: 4, core: 2. Of those that a mesh axis runs over, the one named last changes fastest.
Arguments:
- slc: bfloat16 [2, 64, 128, 1024], P(None, ('groups', 'epoch'), 'space', 'sub'), parts along dimension 1, may hold values from -8 to 8
- offsets: int32 [64, 4], P(('groups', 'epoch')), parts along dimension 0, may hold values from 1 to 8, as said below
- weights: float32 [64, 4], P(('groups', 'epoch')), parts along dimension 0, may hold values from 0.3 to 3
- estimate: float32 [64, 32, 1024], P(('groups', 'epoch'), 'space', 'sub'), parts along dimension 0, may hold values from -2 to 2
- direction: float32 [64, 32, 1024], P(('groups', 'epoch'), 'space', 'sub'), parts along dimension 0, may hold values from -2 to 2
- prev_mean: float32 [1], replicated, may hold values from 0.05 to 0.5
Outputs:
- new_estimate: float32 [64, 32, 1024], P(('groups', 'epoch'), 'space', 'sub'), parts along dimension 0
- new_direction: float32 [64, 32, 1024], P(('groups', 'epoch'), 'space', 'sub'), parts along dimension 0
There are 2 independent parts, one for each index of `groups`. A program takes and returns all parts, laid end to end along the dimension named above; an argument that names none is the same for every part. Nothing has to cross between parts.
Inputs may be any that keep to these rules, and one draw needn't show every extreme that they name: `offsets`: each row holds 4 different distances; partners wrap past the last epoch to the first.
All inputs are finite; a program needn't handle non-finite values.
Results may differ from a plain program's by a relative error of at most 0.0003.
Values may be sent and summed in bfloat16 or wider, within the bound.
A program may use at most 64 MiB of HBM per device.

v0:
```python
import jax
import jax.numpy as jnp
from jax import lax
from jax.sharding import PartitionSpec as P

SLOTS = 4
OFFS = 8
LOOK = 4
RADIUS = 3


EPSILON = 1e-06


def passed_along(x, axis, by):
    size = lax.axis_size(axis)
    return lax.ppermute(x, axis, [(i, (i + by) % size) for i in range(size)])


def extended_2(block, sides, width):
    for axis, dim in sides:
        count = lax.axis_size(axis)
        forward = [(i, i + 1) for i in range(count - 1)]
        backward = [(target, source) for source, target in forward]
        low = lax.ppermute(
            lax.slice_in_dim(block, block.shape[dim] - width, None, axis=dim), axis, forward
        )
        high = lax.ppermute(lax.slice_in_dim(block, 0, width, axis=dim), axis, backward)
        block = jnp.concatenate([low, block, high], axis=dim)
    return block


def looked_sum(field):
    shape = field.shape
    return jnp.sum(field.reshape(shape[:-2] + (shape[-2] // LOOK, LOOK, shape[-1])), axis=-2)


def window_sum(padded, axis):
    length = padded.shape[axis] - 2 * RADIUS
    total = lax.slice_in_dim(padded, 0, length, axis=axis)
    for shift_at in range(1, 2 * RADIUS + 1):
        total = total + lax.slice_in_dim(padded, shift_at, shift_at + length, axis=axis)
    return total


def on_device(slc, offsets, weights, estimate, direction, prev_mean):
    epochs_here = slc.shape[1]
    look_rows = slc.shape[2] // LOOK
    col_count = slc.shape[3]
    ahead = passed_along(slc, "epoch", -1)
    extended = jnp.concatenate([slc, ahead], axis=1)
    numbers = jnp.arange(epochs_here, dtype=jnp.int32)
    partner = numbers[:, None] + offsets
    own_real = slc[0].astype(jnp.float32)
    own_imag = slc[1].astype(jnp.float32)
    ext_real = extended[0].astype(jnp.float32)
    ext_imag = extended[1].astype(jnp.float32)
    powers = looked_sum(ext_real * ext_real + ext_imag * ext_imag)
    pieces = []
    for slot_index in range(SLOTS):
        mate_real = jnp.take(ext_real, partner[:, slot_index], axis=0)
        mate_imag = jnp.take(ext_imag, partner[:, slot_index], axis=0)
        pieces.append(looked_sum(own_real * mate_real + own_imag * mate_imag))
        pieces.append(looked_sum(own_imag * mate_real - own_real * mate_imag))
    pair_count = epochs_here * 2 * SLOTS
    stacked = jnp.concatenate(
        [jnp.stack(pieces, axis=1).reshape(pair_count, look_rows, col_count), powers], axis=0
    )
    padded = extended_2(stacked, (("space", 1), ("sub", 2)), RADIUS)
    boxed = window_sum(window_sum(padded, 1), 2)
    pair_boxed = boxed[:pair_count].reshape(epochs_here, 2 * SLOTS, look_rows, col_count)
    power_box = boxed[pair_count:]
    coh_real = pair_boxed[:, 0::2]
    coh_imag = pair_boxed[:, 1::2]
    denominator = power_box[:epochs_here, None] * jnp.take(power_box, partner, axis=0) + EPSILON
    coherence = (coh_real * coh_real + coh_imag * coh_imag) / denominator
    observed = coh_imag / jnp.sqrt(denominator)
    est_ahead = passed_along(estimate, "epoch", -1)
    est_extended = jnp.concatenate([estimate, est_ahead], axis=0)
    fitted = estimate[:, None] - jnp.take(est_extended, partner, axis=0)
    factor = weights[:, :, None, None] * coherence
    weighted = factor * (observed - fitted)
    flattened = weighted.reshape(epochs_here * SLOTS, look_rows * col_count)
    selector = (
        jnp.arange(epochs_here + OFFS, dtype=jnp.int32)[:, None] == partner.reshape(1, -1)
    ).astype(jnp.float32)
    gathered = jnp.dot(
        selector, flattened, precision=lax.Precision.HIGHEST, preferred_element_type=jnp.float32
    ).reshape(epochs_here + OFFS, look_rows, col_count)
    own_part = jnp.sum(weighted, axis=1) - gathered[:epochs_here]
    returned = passed_along(-gathered[epochs_here:], "epoch", 1)
    gradient = jnp.concatenate([own_part + returned, own_part[OFFS:]], axis=0)
    cell_count = float(
        epochs_here
        * lax.axis_size("epoch")
        * look_rows
        * lax.axis_size("space")
        * col_count
        * lax.axis_size("sub")
    )
    local_norm = jnp.sum(gradient * gradient)
    local_crossed = jnp.sum(gradient * direction)
    mean_before = prev_mean[0]
    fields_ahead = passed_along(
        jnp.stack([gradient, direction]).astype(jnp.bfloat16), "epoch", -1
    ).astype(jnp.float32)
    grad_extended = jnp.concatenate([gradient, fields_ahead[0]], axis=0)
    old_extended = jnp.concatenate([direction, fields_ahead[1]], axis=0)
    grad_spread = gradient[:, None] - jnp.take(grad_extended, partner, axis=0)
    old_spread = direction[:, None] - jnp.take(old_extended, partner, axis=0)
    totals = lax.psum(
        (
            local_norm,
            local_crossed,
            jnp.sum(factor * grad_spread * grad_spread),
            jnp.sum(factor * grad_spread * old_spread),
            jnp.sum(factor * old_spread * old_spread),
        ),
        ("epoch", "space", "sub"),
    )
    grad_norm, crossed, grad_term, mixed_term, old_term = totals
    momentum = grad_norm / cell_count / mean_before
    new_direction = gradient + momentum * direction
    curvature = grad_term + 2.0 * momentum * mixed_term + momentum * momentum * old_term
    along_sum = grad_norm + momentum * crossed
    step_size = along_sum / curvature
    return (estimate + step_size * new_direction, new_direction)


def solution(mesh):
    return jax.shard_map(
        on_device,
        mesh=mesh,
        in_specs=(
            P(None, ("groups", "epoch"), "space", "sub"),
            P(("groups", "epoch"), None),
            P(("groups", "epoch"), None),
            P(("groups", "epoch"), "space", "sub"),
            P(("groups", "epoch"), "space", "sub"),
            P(),
        ),
        out_specs=(P(("groups", "epoch"), "space", "sub"), P(("groups", "epoch"), "space", "sub")),
        check_vma=False,
    )
```

profile of v0, /device:TPU:0, one launch (start us, length us, event | category | flops | bytes accessed | tf_op | source)
XLA Modules:
  0.0 223.2 jit_solution(3602358008610256752)
XLA Ops:
  0.6 5.1 %collective-permute-start = (bf16[2,8,64,512]{3,2,1,0:T(8,128)(2,1)}, bf16[2,8,64,512]{3,2,1,0:T(8,128)(2,1)S(1)}, u32[]{:S(2)}, u32[]{:S(2)}) collective-permute-start(bf16[2,8,64,512]{3,2,1,0:T(8,128)(2,1)} %param.10), channel_id=1, source_target_pairs={{0,12},{4,0},{8,4},{12,8},{1,13},{5,1},{9,5},{13,9},{2,14},{6,2},{... | collective-permute-start | bytes 3145736 | tf_op jit(solution)/shard_map/ppermute | solution.py:17
  6.5 1.3 constant_dynamic-update-slice_fusion.1
  7.8 20.7 %collective-permute-done = bf16[2,8,64,512]{3,2,1,0:T(8,128)(2,1)S(1)} collective-permute-done((bf16[2,8,64,512]{3,2,1,0:T(8,128)(2,1)}, bf16[2,8,64,512]{3,2,1,0:T(8,128)(2,1)S(1)}, u32[]{:S(2)}, u32[]{:S(2)}) %collective-permute-start) | collective-permute-done | bytes 1048608 | tf_op jit(solution)/shard_map/ppermute | solution.py:17
  28.6 1.7 fusion
  30.3 1.9 convert_bitcast_fusion.1
  32.2 3.2 %gather_fusion.5 = f32[8,64,512]{2,1,0:T(8,128)} fusion(f32[16,64,512]{2,1,0:T(8,128)} %get-tuple-element.42, s32[1024]{0:T(1024)S(1)} %get-tuple-element.61), kind=kCustom, calls=%fused_computation.6.clone | custom fusion | bytes 2097184 | tf_op jit(solution)/shard_map/jit(_take)/gather | solution.py:62
  35.4 1.6 gather_fusion.4
  37.0 3.3 %gather_fusion.1 = f32[8,64,512]{2,1,0:T(8,128)} fusion(f32[16,64,512]{2,1,0:T(8,128)} %get-tuple-element.42, s32[1024]{0:T(1024)S(1)} %get-tuple-element.63), kind=kCustom, calls=%fused_computation.2.clone | custom fusion | bytes 2097184 | tf_op jit(solution)/shard_map/jit(_take)/gather | solution.py:62
  40.2 1.6 gather_fusion
  41.8 3.2 %gather_fusion.7 = f32[8,64,512]{2,1,0:T(8,128)} fusion(f32[16,64,512]{2,1,0:T(8,128)} %get-tuple-element.42, s32[1024]{0:T(1024)S(1)} %get-tuple-element.60), kind=kCustom, calls=%fused_computation.8.clone | custom fusion | bytes 2097184 | tf_op jit(solution)/shard_map/jit(_take)/gather | solution.py:62
  45.0 1.6 gather_fusion.6
  46.7 3.2 %gather_fusion.3 = f32[8,64,512]{2,1,0:T(8,128)} fusion(f32[16,64,512]{2,1,0:T(8,128)} %get-tuple-element.42, s32[1024]{0:T(1024)S(1)} %get-tuple-element.62), kind=kCustom, calls=%fused_computation.4.clone | custom fusion | bytes 2097184 | tf_op jit(solution)/shard_map/jit(_take)/gather | solution.py:62
  49.8 1.6 gather_fusion.2
  51.4 1.9 add.120
  53.4 4.8 %fusion.7 = (f32[8,64,512]{2,1,0:T(8,128)}, f32[8,64,512]{2,1,0:T(8,128)}, f32[8,64,512]{2,1,0:T(8,128)}, f32[8,64,512]{2,1,0:T(8,128)}) fusion(f32[8,64,512]{2,1,0:T(8,128)} %gather_fusion.5, f32[8,64,512]{2,1,0:T(8,128)} %gather_fusion.4, pred[8]{0:T(512)(128)(4,1)S(1)} %get-tuple-element.52, bf16[2,8,64,512]{3,2,1,0:T(8,128)(2,1)S(1)} %copy-done.1, ...), kind=kLoop, calls=%fused_computation.53 | loop fusion | flops 4718592 | bytes 9437200 | tf_op jit(solution)/shard_map/sub | solution.py:64
  58.2 2.5 %reshape.74 = f32[8,16,4,512]{3,2,1,0:T(4,128)} reshape(f32[8,64,512]{2,1,0:T(8,128)} %get-tuple-element.45) | data formatting | bytes 2097152 | tf_op jit(solution)/shard_map/reshape | solution.py:35
  60.8 2.2 reduce_sum.143
  62.9 1.9 reduce_sum.135
  64.8 2.5 %reshape.75 = f32[8,16,4,512]{3,2,1,0:T(4,128)} reshape(f32[8,64,512]{2,1,0:T(8,128)} %get-tuple-element.46) | data formatting | bytes 2097152 | tf_op jit(solution)/shard_map/reshape | solution.py:35
  67.3 1.9 reduce_sum.136
  69.2 4.8 %fusion.9 = (f32[8,64,512]{2,1,0:T(8,128)}, f32[8,64,512]{2,1,0:T(8,128)}, f32[8,64,512]{2,1,0:T(8,128)}, f32[8,64,512]{2,1,0:T(8,128)}) fusion(f32[8,64,512]{2,1,0:T(8,128)} %gather_fusion.7, f32[8,64,512]{2,1,0:T(8,128)} %gather_fusion.6, pred[8]{0:T(512)(128)(4,1)S(1)} %get-tuple-element.21, bf16[2,8,64,512]{3,2,1,0:T(8,128)(2,1)S(1)} %copy-done.1, ...), kind=kLoop, calls=%fused_computation.55 | loop fusion | flops 4718592 | bytes 9437200 | tf_op jit(solution)/shard_map/sub | solution.py:64
  74.0 2.6 %reshape.76 = f32[8,16,4,512]{3,2,1,0:T(4,128)} reshape(f32[8,64,512]{2,1,0:T(8,128)} %get-tuple-element.43) | data formatting | bytes 2097152 | tf_op jit(solution)/shard_map/reshape | solution.py:35
  76.6 2.6 %reduce_sum.137 = f32[8,16,512]{2,1,0:T(8,128)} reduce(f32[8,16,4,512]{3,2,1,0:T(4,128)} %reshape.76, f32[]{:T(128)} %constant.20.clone.1), dimensions={2}, to_apply=%region_2.4 | reduce | flops 196608 | bytes 1310724 | tf_op jit(solution)/shard_map/reduce_sum | solution.py:35
  79.2 1.3 reshape.77
  80.5 2.7 %reduce_sum.138 = f32[8,16,512]{2,1,0:T(8,128)} reduce(f32[8,16,4,512]{3,2,1,0:T(4,128)} %reshape.77, f32[]{:T(128)} %constant.20.clone.1), dimensions={2}, to_apply=%region_3.5 | reduce | flops 196608 | bytes 1310724 | tf_op jit(solution)/shard_map/reduce_sum | solution.py:35
  83.1 2.5 %reshape.78 = f32[8,16,4,512]{3,2,1,0:T(4,128)} reshape(f32[8,64,512]{2,1,0:T(8,128)} %get-tuple-element.34) | data formatting | bytes 2097152 | tf_op jit(solution)/shard_map/reshape | solution.py:35
  85.7 2.6 %reduce_sum.139 = f32[8,16,512]{2,1,0:T(8,128)} reduce(f32[8,16,4,512]{3,2,1,0:T(4,128)} %reshape.78, f32[]{:T(128)} %constant.20.clone.1), dimensions={2}, to_apply=%region_4.6 | reduce | flops 196608 | bytes 1310724 | tf_op jit(solution)/shard_map/reduce_sum | solution.py:35
  88.2 1.3 reshape.79
  89.5 2.7 %reduce_sum.140 = f32[8,16,512]{2,1,0:T(8,128)} reduce(f32[8,16,4,512]{3,2,1,0:T(4,128)} %reshape.79, f32[]{:T(128)} %constant.20.clone.1), dimensions={2}, to_apply=%region_5.7 | reduce | flops 196608 | bytes 1310724 | tf_op jit(solution)/shard_map/reduce_sum | solution.py:35
  92.2 2.5 %reshape.80 = f32[8,16,4,512]{3,2,1,0:T(4,128)} reshape(f32[8,64,512]{2,1,0:T(8,128)} %get-tuple-element.32) | data formatting | bytes 2097152 | tf_op jit(solution)/shard_map/reshape | solution.py:35
  94.7 2.5 %reduce_sum.141 = f32[8,16,512]{2,1,0:T(8,128)} reduce(f32[8,16,4,512]{3,2,1,0:T(4,128)} %reshape.80, f32[]{:T(128)} %constant.20.clone.1), dimensions={2}, to_apply=%region_6.8 | reduce | flops 196608 | bytes 1310724 | tf_op jit(solution)/shard_map/reduce_sum | solution.py:35
  97.2 1.3 reshape.81
  98.5 2.6 %reduce_sum.142 = f32[8,16,512]{2,1,0:T(8,128)} reduce(f32[8,16,4,512]{3,2,1,0:T(4,128)} %reshape.81, f32[]{:T(128)} %constant.20.clone.1), dimensions={2}, to_apply=%region_7.9 | reduce | flops 196608 | bytes 1310724 | tf_op jit(solution)/shard_map/reduce_sum | solution.py:35
  101.2 1.1 bitcast_dynamic-update-slice_fusion.5
  103.1 1.5 collective-permute-start.2
  104.5 0.9 copy.55
  105.5 5.9 %collective-permute-start.1 = (f32[80,3,512]{2,0,1:T(8,128)}, f32[80,3,512]{2,0,1:T(8,128)}, u32[]{:S(2)}, u32[]{:S(2)}) collective-permute-start(f32[80,3,512]{2,0,1:T(8,128)} %copy.55), channel_id=1, source_target_pairs={{0,2},{1,3},{4,6},{5,7},{8,10},{9,11},{12,14},{13,15},{16,18},{17,... | collective-permute-start | bytes 1474568 | tf_op jit(solution)/shard_map/ppermute | solution.py:25
  111.4 4.2 %collective-permute-start.5 = (f32[8,16,512]{2,1,0:T(8,128)S(1)}, f32[8,16,512]{2,1,0:T(8,128)}, u32[]{:S(2)}, u32[]{:S(2)}) collective-permute-start(f32[8,16,512]{2,1,0:T(8,128)S(1)} %copy-done.8), channel_id=1, source_target_pairs={{0,12},{4,0},{8,4},{12,8},{1,13},{5,1},{9,5},{13,9},{2,14},{6,2},{... | collective-permute-start | bytes 786440 | tf_op jit(solution)/shard_map/ppermute | solution.py:17
  116.1 1.1 collective-permute-done.2
  117.2 1.4 copy.58
  118.5 1.7 collective-permute-done.1
  120.3 1.4 copy.57
  121.6 1.9 pad_maximum_fusion.4
  123.5 2.2 copy.60
  125.7 1.3 collective-permute-start.4
  126.9 2.2 copy.59
  129.1 4.2 %collective-permute-start.3 = (f32[80,22,3]{0,1,2:T(8,128)}, f32[80,22,3]{0,1,2:T(8,128)}, u32[]{:S(2)}, u32[]{:S(2)}) collective-permute-start(f32[80,22,3]{0,1,2:T(8,128)} %copy.59), channel_id=1, source_target_pairs={{0,1},{2,3},{4,5},{6,7},{8,9},{10,11},{12,13},{14,15},{16,17},{18,... | collective-permute-start | bytes 63368 | tf_op jit(solution)/shard_map/ppermute | solution.py:25
  133.3 1.8 pad_maximum_fusion.7
  135.1 2.7 %gather_fusion.9 = f32[32,16,512]{2,1,0:T(8,128)} fusion(f32[16,16,512]{2,1,0:T(8,128)} %pad_maximum_fusion.7, s32[1024]{0:T(1024)S(1)} %pad_clamp_fusion), kind=kCustom, calls=%fused_computation.9.clone | custom fusion | bytes 2097280 | tf_op jit(solution)/shard_map/jit(_take)/gather | solution.py:80
  137.8 2.1 copy.62
  139.9 2.1 copy.61
  142.0 6.8 %pad_maximum_fusion = f32[80,22,518]{2,1,0:T(8,128)S(1)} fusion(f32[80,22,3]{2,1,0:T(8,128)} %copy.62, f32[80,3,512]{2,1,0:T(4,128)S(1)} %copy.58, f32[16,16,512]{2,1,0:T(8,128)S(1)} %copy-done.2, f32[64,16,512]{2,1,0:T(8,128)S(1)} %bitcast.80, f32[80,3,512]{2,1,0:T(4,128)} %copy-done.3, f32[80,22,3]{2,1,0:T(8,128)} %copy.61), kind=kLoop, calls=%fused_computation.12 | loop fusion | flops 4558400 | bytes 7293440 | tf_op jit(solution)/shard_map/concatenate | solution.py:29
  148.8 2.0 slice_add_fusion
  150.8 4.2 %slice_add_fusion.6 = f32[80,16,512]{2,1,0:T(8,128)S(1)} fusion(f32[80,16,518]{2,1,0:T(8,128)S(1)} %slice_add_fusion), kind=kLoop, calls=%fused_computation.39 | loop fusion | flops 3932160 | bytes 20971520 | tf_op jit(solution)/shard_map/add | solution.py:42
  155.0 1.6 slice.190
  157.3 1.6 gather_fusion.8
  158.9 2.8 %fusion.17 = (f32[8,16,512]{2,1,0:T(8,128)S(1)}, f32[8,4,16,512]{3,2,1,0:T(8,128)S(1)}, f32[8,4,16,512]{3,2,1,0:T(8,128)S(1)}) fusion(f32[8,16,512]{2,1,0:T(8,128)S(1)} %copy-done.8, pred[8,4]{1,0:T(8,128)(4,1)S(1)} %copy.63, f32[8,16,512]{2,1,0:T(8,128)S(1)} %slice-done, f32[8,8,16,512]{3,2,1,0:T(8,128)} %bitcast.81, f32[8,4]{1,0:T(8,128)S(1)} %copy.54, ...), kind=kLoop, calls=%fused_computation.116 | loop fusion | flops 3604480 | bytes 7078048 | tf_op jit(solution)/shard_map/reduce_sum | solution.py:90
  163.4 9.1 %collective-permute-done.6 = f32[8,16,512]{2,1,0:T(8,128)S(1)} collective-permute-done((f32[8,16,512]{2,1,0:T(8,128)S(1)}, f32[8,16,512]{2,1,0:T(8,128)S(1)}, u32[]{:S(2)}, u32[]{:S(2)}) %collective-permute-start.6) | collective-permute-done | bytes 262176 | tf_op jit(solution)/shard_map/ppermute | solution.py:17
  173.5 1.7 collective-permute-start.7
  175.9 4.0 %collective-permute-done.7 = bf16[2,8,16,512]{3,2,1,0:T(8,128)(2,1)S(1)} collective-permute-done((bf16[2,8,16,512]{3,2,1,0:T(8,128)(2,1)S(1)}, bf16[2,8,16,512]{3,2,1,0:T(8,128)(2,1)S(1)}, u32[]{:S(2)}, u32[]{:S(2)}) %collective-permute-start.7) | collective-permute-done | bytes 262176 | tf_op jit(solution)/shard_map/ppermute | solution.py:17
  181.4 1.0 pad_maximum_fusion.8
  182.4 1.6 gather_fusion.10
  184.0 2.4 %fusion.1 = (f32[]{:T(128)}, f32[]{:T(128)}, f32[]{:T(128)}) fusion(f32[8,4,16,512]{3,2,1,0:T(8,128)S(1)} %get-tuple-element.20, f32[8,4,16,512]{3,2,1,0:T(8,128)S(1)} %bitcast.82, f32[8,16,512]{2,1,0:T(8,128)S(1)} %copy-done.7, pred[8,4]{1,0:T(8,128)(4,1)S(1)} %copy.63, f32[8,4,16,512]{3,2,1,0:T(8,128)} %bitcast.83, f32[8,16,512]{2,1,0:T(8,128)S(1)} %get-tuple-element.17), kind=kLoop, calls=%fused_computation.47 | loop fusion | flops 3145725 | bytes 3670060 | tf_op jit(solution)/shard_map/reduce_sum | solution.py:117
  186.4 32.0 %all-reduce = (f32[]{:T(128)}, f32[]{:T(128)}, f32[]{:T(128)}, f32[]{:T(128)}, f32[]{:T(128)}) all-reduce(f32[]{:T(128)} %get-tuple-element.8, f32[]{:T(128)} %get-tuple-element.7, f32[]{:T(128)} %get-tuple-element.6, f32[]{:T(128)} %get-tuple-element.5, ...), channel_id=1, replica_groups=mesh['groups'=2,'epoch'=4,'space'=2,'sub'=2] {'epoch','space','sub'}, use_global_device_ids=true, to_apply=%region_11.14 | all-reduce | flops 5 | bytes 40 | tf_op jit(solution)/shard_map/psum | solution.py:111
  (73 shorter events, 7.6 us)
Async XLA Ops:
  0.6 27.9 %collective-permute-start = (bf16[2,8,64,512]{3,2,1,0:T(8,128)(2,1)}, bf16[2,8,64,512]{3,2,1,0:T(8,128)(2,1)S(1)}, u32[]{:S(2)}, u32[]{:S(2)}) collective-permute-start(bf16[2,8,64,512]{3,2,1,0:T(8,128)(2,1)} %param.10), channel_id=1, source_target_pairs={{0,12},{4,0},{8,4},{12,8},{1,13},{5,1},{9,5},{13,9},{2,14},{6,2},{... | collective-permute-start | bytes 3145736 | tf_op jit(solution)/shard_map/ppermute | solution.py:17
  51.4 2.0 copy-start.1
  74.0 5.2 %copy-start.6 = (f32[8,64,512]{2,1,0:T(8,128)S(1)}, f32[8,64,512]{2,1,0:T(8,128)}, u32[]{:S(2)}) copy-start(f32[8,64,512]{2,1,0:T(8,128)} %get-tuple-element.44) | copy-start | bytes 3145732
  80.5 7.7 %copy-start.4 = (f32[8,64,512]{2,1,0:T(8,128)S(1)}, f32[8,64,512]{2,1,0:T(8,128)}, u32[]{:S(2)}) copy-start(f32[8,64,512]{2,1,0:T(8,128)} %get-tuple-element.33) | copy-start | bytes 3145732
  89.5 7.7 %copy-start.5 = (f32[8,64,512]{2,1,0:T(8,128)S(1)}, f32[8,64,512]{2,1,0:T(8,128)}, u32[]{:S(2)}) copy-start(f32[8,64,512]{2,1,0:T(8,128)} %get-tuple-element.31) | copy-start | bytes 3145732
  98.5 3.8 %copy-start.9 = (f32[8,16,512]{2,1,0:T(8,128)S(1)}, f32[8,16,512]{2,1,0:T(8,128)}, u32[]{:S(2)}) copy-start(f32[8,16,512]{2,1,0:T(8,128)} %reduce_sum.138) | copy-start | bytes 786436
  98.5 3.8 %copy-start.10 = (f32[8,16,512]{2,1,0:T(8,128)S(1)}, f32[8,16,512]{2,1,0:T(8,128)}, u32[]{:S(2)}) copy-start(f32[8,16,512]{2,1,0:T(8,128)} %reduce_sum.139) | copy-start | bytes 786436
  101.2 1.2 copy-start.11
  101.2 1.2 copy-start.12
  101.2 1.3 copy-start.13
  101.2 1.4 copy-start.2
  102.9 8.6 %copy-start.8 = (f32[8,16,512]{2,1,0:T(8,128)S(1)}, f32[8,16,512]{2,1,0:T(8,128)}, u32[]{:S(2)}) copy-start(f32[8,16,512]{2,1,0:T(8,128)} %param.13) | copy-start | bytes 786436
  102.9 12.8 %copy-start.14 = (s32[8,4]{0,1:T(4,128)S(1)}, s32[8,4]{0,1:T(4,128)}, u32[]{:S(2)}) copy-start(s32[8,4]{0,1:T(4,128)} %param.11) | copy-start | bytes 388
  102.9 12.9 %copy-start.15 = (f32[8,4]{0,1:T(4,128)S(1)}, f32[8,4]{0,1:T(4,128)}, u32[]{:S(2)}) copy-start(f32[8,4]{0,1:T(4,128)} %param.12) | copy-start | bytes 388
  103.1 14.1 %collective-permute-start.2 = (f32[80,3,512]{2,0,1:T(8,128)S(1)}, f32[80,3,512]{2,0,1:T(8,128)}, u32[]{:S(2)}, u32[]{:S(2)}) collective-permute-start(f32[80,3,512]{2,0,1:T(8,128)S(1)} %copy.56), channel_id=1, source_target_pairs={{2,0},{3,1},{6,4},{7,5},{10,8},{11,9},{14,12},{15,13},{18,16},{19,... | collective-permute-start | bytes 1474568 | tf_op jit(solution)/shard_map/ppermute | solution.py:28
  105.5 14.8 %collective-permute-start.1 = (f32[80,3,512]{2,0,1:T(8,128)}, f32[80,3,512]{2,0,1:T(8,128)}, u32[]{:S(2)}, u32[]{:S(2)}) collective-permute-start(f32[80,3,512]{2,0,1:T(8,128)} %copy.55), channel_id=1, source_target_pairs={{0,2},{1,3},{4,6},{5,7},{8,10},{9,11},{12,14},{13,15},{16,18},{17,... | collective-permute-start | bytes 1474568 | tf_op jit(solution)/shard_map/ppermute | solution.py:25
  111.4 21.9 %collective-permute-start.5 = (f32[8,16,512]{2,1,0:T(8,128)S(1)}, f32[8,16,512]{2,1,0:T(8,128)}, u32[]{:S(2)}, u32[]{:S(2)}) collective-permute-start(f32[8,16,512]{2,1,0:T(8,128)S(1)} %copy-done.8), channel_id=1, source_target_pairs={{0,12},{4,0},{8,4},{12,8},{1,13},{5,1},{9,5},{13,9},{2,14},{6,2},{... | collective-permute-start | bytes 786440 | tf_op jit(solution)/shard_map/ppermute | solution.py:17
  121.6 1.9 copy-start.3
  125.7 12.2 %collective-permute-start.4 = (f32[80,22,3]{0,1,2:T(8,128)}, f32[80,22,3]{0,1,2:T(8,128)}, u32[]{:S(2)}, u32[]{:S(2)}) collective-permute-start(f32[80,22,3]{0,1,2:T(8,128)} %copy.60), channel_id=1, source_target_pairs={{1,0},{3,2},{5,4},{7,6},{9,8},{11,10},{13,12},{15,14},{17,16},{19,... | collective-permute-start | bytes 63368 | tf_op jit(solution)/shard_map/ppermute | solution.py:28
  129.1 10.8 %collective-permute-start.3 = (f32[80,22,3]{0,1,2:T(8,128)}, f32[80,22,3]{0,1,2:T(8,128)}, u32[]{:S(2)}, u32[]{:S(2)}) collective-permute-start(f32[80,22,3]{0,1,2:T(8,128)} %copy.59), channel_id=1, source_target_pairs={{0,1},{2,3},{4,5},{6,7},{8,9},{10,11},{12,13},{14,15},{16,17},{18,... | collective-permute-start | bytes 63368 | tf_op jit(solution)/shard_map/ppermute | solution.py:25
  155.0 2.2 copy-start
  157.2 1.6 slice-start
  162.3 10.4 %copy-start.7 = (f32[8,16,512]{2,1,0:T(8,128)S(1)}, f32[8,16,512]{2,1,0:T(8,128)}, u32[]{:S(2)}) copy-start(f32[8,16,512]{2,1,0:T(8,128)} %param.14) | copy-start | bytes 786436
  163.0 9.5 %collective-permute-start.6 = (f32[8,16,512]{2,1,0:T(8,128)S(1)}, f32[8,16,512]{2,1,0:T(8,128)S(1)}, u32[]{:S(2)}, u32[]{:S(2)}) collective-permute-start(f32[8,16,512]{2,1,0:T(8,128)S(1)} %copy.69), channel_id=1, source_target_pairs={{0,4},{4,8},{8,12},{12,0},{1,5},{5,9},{9,13},{13,1},{2,6},{6,10},{... | collective-permute-start | bytes 786440 | tf_op jit(solution)/shard_map/ppermute | solution.py:17
  173.5 6.4 %collective-permute-start.7 = (bf16[2,8,16,512]{3,2,1,0:T(8,128)(2,1)S(1)}, bf16[2,8,16,512]{3,2,1,0:T(8,128)(2,1)S(1)}, u32[]{:S(2)}, u32[]{:S(2)}) collective-permute-start(bf16[2,8,16,512]{3,2,1,0:T(8,128)(2,1)S(1)} %pad_maximum_fusion.10), channel_id=1, source_target_pairs={{0,12},{4,0},{8,4},{12,8},{1,13},{5,1},{9,5},{13,9},{2,14},{6,2},{... | collective-permute-start | bytes 786440 | tf_op jit(solution)/shard_map/ppermute | solution.py:17
where the time goes:
time: 225 us; the launch traced here: 223 us
  local copies, waits for them, and re-layouts  63.5 us (28%)
  other arithmetic  60.6 us (27%)
  waiting for transfers between devices  36.6 us (16%)
  blocking collectives  32 us (14%)
  starting transfers between devices  24.4 us (11%)
  between operations  5.64 us (3%)
    ppermute x4, waiting for transfers between devices, passed_along(): return lax.ppermute(x, axis, [(i, (i + by) % size) for i in range(size)])  33.8 us
    psum x1, blocking collectives, on_device(): lax.psum((local_norm, local_crossed, jnp.sum(factor * grad_spread * grad_...  32 us
    reduce_sum x9, other arithmetic, looked_sum(): jnp.sum(field.reshape(shape[:-2] + (shape[-2] // LOOK, LOOK, shape[-1])),...  21.5 us
    reshape x8, local copies, waits for them, and re-layouts, looked_sum(): field.reshape(shape[:-2] + (shape[-2] // LOOK, LOOK, shape[-1]))  16.5 us
    gather x4, local copies, waits for them, and re-layouts, on_device(): mate_imag = jnp.take(ext_imag, partner[:, slot_index], axis=0)  12.8 us
    ppermute x4, starting transfers between devices, passed_along(): return lax.ppermute(x, axis, [(i, (i + by) % size) for i in range(size)])  11.5 us
    ppermute x2, starting transfers between devices, extended_2(): lax.ppermute(lax.slice_in_dim(block, block.shape[dim] - width, None, axis...  10.2 us
    sub x2, other arithmetic, on_device(): pieces.append(looked_sum(own_imag * mate_real - own_real * mate_imag))  9.68 us
  transfers between devices with their start and end apart: 8, of which 5 were waited for; matrix products, arithmetic and copies ran while one was open for 8% of the time, Pallas kernels for 0%

commit v1 on v0

v1 whole, which is shorter than its diff:
```python
import functools

import jax
import jax.numpy as jnp
from jax import lax
from jax.experimental import pallas as pl
from jax.experimental.pallas import tpu as pltpu
from jax.sharding import PartitionSpec as P

SLOTS = 4
OFFS = 8
LOOK = 4
RADIUS = 3
EPSILON = 1e-06
LANES = 128
PACK = 16
MESH = pl.DeviceIdType.MESH
F32 = jnp.float32
BF16 = jnp.bfloat16


def windowed(x, axis):
    size = x.shape[axis]
    three = x + pltpu.roll(x, 1, axis) + pltpu.roll(x, size - 1, axis)
    return x + pltpu.roll(three, 2, axis) + pltpu.roll(three, size - 2, axis)


def folded(x):
    total = None
    for row in range(0, x.shape[0], 8):
        for col in range(0, x.shape[1], LANES):
            piece = x[row : row + 8, col : col + LANES]
            total = piece if total is None else total + piece
    return total


def step_kernel(
    sizes,
    slc,
    offsets,
    weights,
    estimate,
    direction,
    prev_mean,
    new_estimate,
    new_direction,
    raw,
    tmp,
    ext,
    pbox,
    est,
    dirs,
    dir_low,
    dir_in,
    acc,
    ret_in,
    own_low,
    own_in,
    grad,
    factors,
    red_c,
    red_x,
    red_z,
    loc_sem,
    misc_sem,
    z_send,
    z_recv,
    e_send,
    e_recv,
    d_sem,
    x_send,
    x_recv,
    c_send,
    c_recv,
    r_send,
    r_recv,
    o_send,
    o_recv,
    rc_send,
    rc_recv,
    rx_send,
    rx_recv,
    rz_send,
    rz_recv,
):
    nz, nx, nc = sizes
    here = slc.shape[1]
    rows = slc.shape[2]
    cols = slc.shape[3]
    total_rows = rows + 2 * PACK
    look_rows = rows // LOOK
    ext_rows = total_rows // LOOK
    rim_rows = PACK // LOOK
    blocks = cols // LANES + 1
    everything = here + OFFS
    z = lax.axis_index("epoch")
    x = lax.axis_index("space")
    c = lax.axis_index("sub")
    z_prev = {"epoch": lax.rem(z + nz - 1, nz)}
    z_next = {"epoch": lax.rem(z + 1, nz)}
    has_next = x < nx - 1
    has_prev = x > 0

    local = [
        pltpu.make_async_copy(estimate, est.at[pl.ds(0, here)], misc_sem.at[0]),
        pltpu.make_async_copy(direction, dirs.at[pl.ds(0, here)], misc_sem.at[1]),
    ]

    def tile_in(b):
        return pltpu.make_async_copy(
            slc.at[:, b], raw.at[b, :, pl.ds(0, rows), pl.ds(0, cols)], loc_sem.at[b]
        )

    local[1].start()
    local[0].start()
    for b in range(here):
        tile_in(b).start()

    barrier = pltpu.get_barrier_semaphore()
    for axis, size, me in (("epoch", nz, z), ("space", nx, x), ("sub", nc, c)):
        for by in range(1, size):
            pl.semaphore_signal(
                barrier, inc=1, device_id={axis: lax.rem(me + by, size)}, device_id_type=MESH
            )
    pl.semaphore_wait(barrier, nz + nx + nc - 3)

    def remote(src, dst, send, recv, device):
        return pltpu.make_async_remote_copy(
            src_ref=src,
            dst_ref=dst,
            send_sem=send,
            recv_sem=recv,
            device_id=device,
            device_id_type=MESH,
        )

    def z_tile(k):
        return remote(
            slc.at[:, k],
            raw.at[here + k, :, pl.ds(0, rows), pl.ds(0, cols)],
            z_send.at[k],
            z_recv.at[k],
            z_prev,
        )

    def z_est(k):
        return remote(estimate.at[k], est.at[here + k], e_send.at[k], e_recv.at[k], z_prev)

    def z_dir():
        return remote(dir_low, dir_in, d_sem.at[0], d_sem.at[1], z_prev)

    def x_down(b, own):
        at = pl.ds(rows - PACK, PACK)
        src = slc.at[:, b, at] if own else raw.at[b, :, at, pl.ds(0, cols)]
        return remote(
            src,
            raw.at[b, :, pl.ds(rows + PACK, PACK), pl.ds(0, cols)],
            x_send.at[0, b],
            x_recv.at[0, b],
            {"space": lax.rem(x + 1, nx)},
        )

    def x_up(b, own):
        at = pl.ds(0, PACK)
        src = slc.at[:, b, at] if own else raw.at[b, :, at, pl.ds(0, cols)]
        return remote(
            src,
            raw.at[b, :, pl.ds(rows, PACK), pl.ds(0, cols)],
            x_send.at[1, b],
            x_recv.at[1, b],
            {"space": lax.rem(x + nx - 1, nx)},
        )

    def c_rim(b):
        start = pl.multiple_of((nc - 1 - c) * (cols - LANES), LANES)
        return remote(
            raw.at[b, :, :, pl.ds(start, LANES)],
            raw.at[b, :, :, pl.ds(cols, LANES)],
            c_send.at[b],
            c_recv.at[b],
            {"sub": lax.rem(c + 1, nc)},
        )

    def x_start(b, own):
        if nx > 1:
            pl.when(has_next)(lambda: x_down(b, own).start())
            pl.when(has_prev)(lambda: x_up(b, own).start())

    def x_wait(b, own):
        if nx > 1:
            pl.when(has_prev)(lambda: x_down(b, own).wait_recv())
            pl.when(has_next)(lambda: x_up(b, own).wait_recv())

    def x_drain(b, own):
        if nx > 1:
            pl.when(has_next)(lambda: x_down(b, own).wait_send())
            pl.when(has_prev)(lambda: x_up(b, own).wait_send())

    def returned(k):
        return remote(acc.at[here + k], ret_in.at[k], r_send.at[k], r_recv.at[k], z_next)

    def owned(k):
        return remote(own_low.at[k], own_in.at[k], o_send.at[k], o_recv.at[k], z_prev)

    for k in range(OFFS):
        x_start(k, True)
    for k in range(OFFS):
        z_est(k).start()
        z_tile(k).start()
    local[1].wait()
    dir_low[...] = dirs[pl.ds(0, OFFS)].astype(BF16)
    acc[...] = jnp.zeros_like(acc)
    local[0].wait()

    row_at = lax.broadcasted_iota(jnp.int32, (ext_rows, LANES), 0)
    lane_at = lax.broadcasted_iota(jnp.int32, (ext_rows, LANES), 1)
    row_first = jnp.where(has_prev, look_rows + rim_rows, ext_rows)
    row_last = jnp.where(has_next, look_rows + rim_rows, look_rows)
    row_ok = (row_at < row_last) | (row_at >= row_first)
    if nc > 1:
        lane_first = jnp.where(c == 0, LANES, LANES - RADIUS)
        lane_last = jnp.where(c == 0, RADIUS, 0)
        rim_ok = row_ok & ((lane_at < lane_last) | (lane_at >= lane_first))
    else:
        rim_ok = row_at < 0

    def boxed(field):
        return windowed(windowed(field, 0)[:look_rows], 1)[:, :cols]

    def prepare(b):
        for part in range(2):
            for v in range(blocks):
                tmp[part, v] = raw[b, part, :, v * LANES : (v + 1) * LANES].astype(F32)
        powers = []
        for v in range(blocks):
            keep = rim_ok if v == blocks - 1 else row_ok
            power = jnp.zeros((ext_rows, LANES), F32)
            for part in range(2):
                for look in range(LOOK):
                    value = tmp[part, v, pl.ds(look, ext_rows, stride=LOOK), :]
                    value = jnp.where(keep, value, 0.0)
                    ext[b, part, look, :, v * LANES : (v + 1) * LANES] = value
                    power = power + value * value
            powers.append(power)
        pbox[b] = boxed(jnp.concatenate(powers, axis=1))

    def pair(e, b):
        real = jnp.zeros((ext_rows, blocks * LANES), F32)
        imag = jnp.zeros((ext_rows, blocks * LANES), F32)
        for look in range(LOOK):
            own_real = ext[e, 0, look]
            own_imag = ext[e, 1, look]
            mate_real = ext[b, 0, look]
            mate_imag = ext[b, 1, look]
            real = real + (own_real * mate_real + own_imag * mate_imag)
            imag = imag + (own_imag * mate_real - own_real * mate_imag)
        real = boxed(real)
        imag = boxed(imag)
        distance = b - e
        weight = jnp.float32(0.0)
        for slot in range(SLOTS):
            weight = weight + jnp.where(
                offsets[e, slot] == distance, weights[e, slot], jnp.float32(0.0)
            )
        root = 1.0 / jnp.sqrt(pbox[e] * pbox[b] + EPSILON)
        real = real * root
        imag = imag * root
        factor = weight * (real * real + imag * imag)
        factors[e * (OFFS + 1) + distance] = factor
        weighted = factor * (imag - (est[e] - est[b]))
        acc[e] = acc[e] + weighted
        acc[b] = acc[b] - weighted

    def pairs_of(b):
        @pl.loop(lax.max(b - OFFS, 0), lax.min(b, here))
        def _(e):
            pair(e, b)

    def settle(b):
        k = b - here
        c_rim(b).wait_recv()
        prepare(b)
        z_est(k).wait_recv()
        pairs_of(b)
        own_low[k] = acc[k].astype(BF16)
        returned(k).start()
        owned(k).start()

    @pl.loop(0, here)
    def _(b):
        tile_in(b).wait()
        x_wait(b, True)
        c_rim(b).start()

        @pl.when(b > 0)
        def _():
            c_rim(b - 1).wait_recv()
            prepare(b - 1)
            pairs_of(b - 1)

    z_dir().start()
    c_rim(here - 1).wait_recv()
    prepare(here - 1)
    pairs_of(here - 1)

    @pl.loop(0, OFFS)
    def _(k):
        b = k + here
        z_tile(k).wait_recv()
        x_start(b, False)

        @pl.when(k > 0)
        def _():
            settle(b - 1)

        x_wait(b, False)
        c_rim(b).start()

    settle(everything - 1)

    z_dir().wait_recv()
    dirs[pl.ds(here, OFFS)] = dir_in[...].astype(F32)
    zero = jnp.zeros((8, LANES), F32)

    @pl.loop(OFFS, here)
    def _(k):
        grad[k] = acc[k]

    @pl.loop(0, OFFS)
    def _(k):
        returned(k).wait_recv()
        owned(k).wait_recv()
        grad[k] = acc[k] + ret_in[k]
        grad[here + k] = own_in[k].astype(F32) + acc[here + k]

    def one_epoch(e, sums):
        norm, crossed, gg, gd, dd = sums
        g = grad[e]
        d = dirs[e]
        norm = norm + folded(g * g)
        crossed = crossed + folded(g * d)
        for slot in range(SLOTS):
            far = offsets[e, slot]
            f = factors[e * (OFFS + 1) + far]
            dg = g - grad[e + far]
            ds = d - dirs[e + far]
            fg = f * dg
            gg = gg + folded(fg * dg)
            gd = gd + folded(fg * ds)
            dd = dd + folded(f * ds * ds)
        return norm, crossed, gg, gd, dd

    sums = lax.fori_loop(0, here, one_epoch, (zero,) * 5)
    tile_row = lax.broadcasted_iota(jnp.int32, (8, LANES), 0)
    tile = zero
    for index, value in enumerate(sums):
        whole = jnp.sum(jnp.sum(value, axis=0, keepdims=True), axis=1, keepdims=True)
        tile = jnp.where(tile_row == index, whole, tile)

    for axis, size, me, red, send, recv in (
        ("sub", nc, c, red_c, rc_send, rc_recv),
        ("space", nx, x, red_x, rx_send, rx_recv),
        ("epoch", nz, z, red_z, rz_send, rz_recv),
    ):
        if size == 1:
            continue
        red[me] = tile

        def share(by, source):
            return remote(
                red.at[source],
                red.at[source],
                send.at[by],
                recv.at[source],
                {axis: lax.rem(me + by, size)},
            )

        for by in range(1, size):
            share(by, me).start()
        for by in range(1, size):
            share(by, lax.rem(me + size - by, size)).wait_recv()
        for by in range(1, size):
            share(by, me).wait_send()
        tile = red[0]
        for source in range(1, size):
            tile = tile + red[source]

    grad_norm, crossed, grad_term, mixed_term, old_term = (tile[i : i + 1, 0:1] for i in range(5))
    cell_count = float(here * nz * look_rows * nx * cols * nc)
    momentum = grad_norm / cell_count / prev_mean[0]
    curvature = grad_term + 2.0 * momentum * mixed_term + momentum * momentum * old_term
    step = (grad_norm + momentum * crossed) / curvature

    @pl.loop(0, here)
    def _(e):
        moved = grad[e] + momentum * dirs[e]
        new_direction[e] = moved
        new_estimate[e] = est[e] + step * moved

    @pl.loop(0, OFFS)
    def _(k):
        z_tile(k).wait_send()
        z_est(k).wait_send()
        returned(k).wait_send()
        owned(k).wait_send()

    @pl.loop(0, here)
    def _(b):
        x_drain(b, True)

    @pl.loop(here, everything)
    def _(b):
        x_drain(b, False)

    @pl.loop(0, everything)
    def _(b):
        c_rim(b).wait_send()

    z_dir().wait_send()


def on_device(sizes, slc, offsets, weights, estimate, direction, prev_mean):
    nz, nx, nc = sizes
    here, rows, cols = slc.shape[1:]
    look_rows = rows // LOOK
    every = here + OFFS
    total_rows = rows + 2 * PACK
    ext_rows = total_rows // LOOK
    wide = cols + LANES
    grid_cell = (look_rows, cols)
    dma = pltpu.SemaphoreType.DMA
    scratch = [
        pltpu.VMEM((every, 2, total_rows, wide), BF16),
        pltpu.VMEM((2, wide // LANES, total_rows, LANES), F32),
        pltpu.VMEM((every, 2, LOOK, ext_rows, wide), F32),
        pltpu.VMEM((every,) + grid_cell, F32),
        pltpu.VMEM((every,) + grid_cell, F32),
        pltpu.VMEM((every,) + grid_cell, F32),
        pltpu.VMEM((OFFS,) + grid_cell, BF16),
        pltpu.VMEM((OFFS,) + grid_cell, BF16),
        pltpu.VMEM((every,) + grid_cell, F32),
        pltpu.VMEM((OFFS,) + grid_cell, F32),
        pltpu.VMEM((OFFS,) + grid_cell, BF16),
        pltpu.VMEM((OFFS,) + grid_cell, BF16),
        pltpu.VMEM((every,) + grid_cell, F32),
        pltpu.VMEM((here * (OFFS + 1),) + grid_cell, F32),
        pltpu.VMEM((nc, 8, LANES), F32),
        pltpu.VMEM((nx, 8, LANES), F32),
        pltpu.VMEM((nz, 8, LANES), F32),
        dma((here,)),
        dma((2,)),
        dma((OFFS,)),
        dma((OFFS,)),
        dma((OFFS,)),
        dma((OFFS,)),
        dma((2,)),
        dma((2, every)),
        dma((2, every)),
        dma((every,)),
        dma((every,)),
        dma((OFFS,)),
        dma((OFFS,)),
        dma((OFFS,)),
        dma((OFFS,)),
        dma((nc,)),
        dma((nc,)),
        dma((nx,)),
        dma((nx,)),
        dma((nz,)),
        dma((nz,)),
    ]
    anywhere = pl.BlockSpec(memory_space=pl.ANY)
    scalars = pl.BlockSpec(memory_space=pltpu.SMEM)
    vectors = pl.BlockSpec(memory_space=pltpu.VMEM)
    out = jax.ShapeDtypeStruct(estimate.shape, F32)
    return tuple(
        pl.pallas_call(
            functools.partial(step_kernel, sizes),
            name="cg_step",
            out_shape=(out, out),
            in_specs=[anywhere, scalars, scalars, anywhere, anywhere, scalars],
            out_specs=(vectors, vectors),
            scratch_shapes=scratch,
            compiler_params=pltpu.CompilerParams(
                collective_id=0, has_side_effects=True, vmem_limit_bytes=60 * 1024 * 1024
            ),
        )(slc, offsets, weights, estimate, direction, prev_mean)
    )


def solution(mesh):
    sizes = (mesh.shape["epoch"], mesh.shape["space"], mesh.shape["sub"])
    tile = P(("groups", "epoch"), "space", "sub")
    rows = P(("groups", "epoch"), None)
    return jax.shard_map(
        functools.partial(on_device, sizes),
        mesh=mesh,
        in_specs=(P(None, ("groups", "epoch"), "space", "sub"), rows, rows, tile, tile, P()),
        out_specs=(tile, tile),
        check_vma=False,
    )
```

time: 225 us -> 68 us (0.30)
  Pallas kernels: 0 us -> 62 us
  other arithmetic: 60.6 us -> 0 us
  local copies, waits for them, and re-layouts: 63.5 us -> 4.45 us
  waiting for transfers between devices: 36.6 us -> 0 us
  blocking collectives: 32 us -> 0 us
  starting transfers between devices: 24.4 us -> 0 us
  between operations: 5.64 us -> 1.3 us
    pallas_call x0 -> x1, Pallas kernels: none -> 62 us  [on_device(): pl.pallas_call(functools.partial(step_kernel, sizes), name='cg_step', out...]
    ppermute x8 -> x0, waiting for transfers between devices: 36.6 us -> none  [the longest x4 33.8 us: passed_along(): return lax.ppermute(x, axis, [(i, (i + by) % size) for i in range(size)])]
    psum x1 -> x0, blocking collectives: 32 us -> none  [on_device(): lax.psum((local_norm, local_crossed, jnp.sum(factor * grad_spread * grad_...]
    reduce_sum x12 -> x0, other arithmetic: 27.4 us -> none  [the longest x9 21.5 us: looked_sum(): jnp.sum(field.reshape(shape[:-2] + (shape[-2] // LOOK, LOOK, shape[-1])),...]
    gather x12 -> x0, local copies, waits for them, and re-layouts: 25.7 us -> none  [the longest x4 12.8 us: on_device(): mate_imag = jnp.take(ext_imag, partner[:, slot_index], axis=0)]
    ppermute x8 -> x0, starting transfers between devices: 24.4 us -> none  [the longest x4 11.5 us: passed_along(): return lax.ppermute(x, axis, [(i, (i + by) % size) for i in range(size)])]
    reshape x8 -> x0, local copies, waits for them, and re-layouts: 16.5 us -> none  [looked_sum(): field.reshape(shape[:-2] + (shape[-2] // LOOK, LOOK, shape[-1]))]
    sub x2 -> x0, other arithmetic: 9.68 us -> none  [on_device(): pieces.append(looked_sum(own_imag * mate_real - own_real * mate_imag))]
  transfers between devices with their start and end apart: 8 -> 0, of which waited for: 5 -> 0; matrix products, arithmetic and copies ran while one was open for 8% -> 0% of each run, Pallas kernels for 0% -> 0%
where the time goes in v1:
time: 68 us; the launch traced here: 67.8 us
  Pallas kernels  62 us (91%)
  local copies, waits for them, and re-layouts  4.45 us (7%)
  between operations  1.3 us (2%)
    pallas_call x1, Pallas kernels, on_device(): pl.pallas_call(functools.partial(step_kernel, sizes), name='cg_step', out...  62 us
    unnamed x8, local copies, waits for them, and re-layouts  4.45 us

profile of v1, /device:TPU:0, one launch (start us, length us, event | category | flops | bytes accessed | tf_op | source)
XLA Modules:
  0.0 67.8 jit_solution(16537598171010147978)
XLA Ops:
  1.3 0.0 copy-start.1
  1.3 1.4 %copy.8.offsets = s32[8,4]{1,0:T(8,128)} copy(s32[8,4]{0,1:T(4,128)} %param.7) | data formatting | bytes 256 | tf_op args[1]
  2.6 0.0 copy-done.1
  2.6 0.7 copy.9.weights
  3.3 62.0 %cg_step.1 = (f32[8,16,512]{2,1,0:T(8,128)}, f32[8,16,512]{2,1,0:T(8,128)}) custom-call(bf16[2,8,64,512]{3,2,1,0:T(8,128)(2,1)} %slc.1, s32[8,4]{1,0:T(8,128)} %copy.8.offsets, f32[8,4]{1,0:T(8,128)} %copy.9.weights, f32[8,16,512]{2,1,0:T(8,128)} %estimate.1, f32[8,16,512]{2,1,0:T(8,128)} %direction.1, f32[1]{0:T(128)S(6)} %copy.12.prev_mean), custom_call_target="tpu_custom_call" | custom-call | tf_op jit(solution)/shard_map/cg_step/pallas_call | solution.py:477
  65.3 0.0 copy-start
  65.3 1.7 %copy.13 = f32[8,16,512]{2,1,0:T(8,128)} copy(f32[8,16,512]{2,1,0:T(8,128)} %get-tuple-element.4) | data formatting | bytes 524288
  67.0 0.0 copy-done
  67.1 0.7 %copy.14 = f32[8,16,512]{2,1,0:T(8,128)} copy(f32[8,16,512]{2,1,0:T(8,128)S(1)} %copy-done) | data formatting | bytes 524288
Async XLA Ops:
  1.3 1.4 %copy-start.1 = (f32[8,4]{0,1:T(4,128)S(1)}, f32[8,4]{0,1:T(4,128)}, u32[]{:S(2)}) copy-start(f32[8,4]{0,1:T(4,128)} %param.8) | copy-start | bytes 388
  65.3 1.7 %copy-start = (f32[8,16,512]{2,1,0:T(8,128)S(1)}, f32[8,16,512]{2,1,0:T(8,128)}, u32[]{:S(2)}) copy-start(f32[8,16,512]{2,1,0:T(8,128)} %get-tuple-element.5) | copy-start | bytes 786436

commit v2 on v1

--- a/solution.py
+++ b/solution.py
@@ -13,6 +13,7 @@
 RADIUS = 3
 EPSILON = 1e-06
 LANES = 128
+LAG = 3
 PACK = 16
 MESH = pl.DeviceIdType.MESH
 F32 = jnp.float32
@@ -37,13 +38,14 @@
 def step_kernel(
     sizes,
     slc,
+    offsets_in,
+    weights_in,
+    estimate,
+    direction,
+    gradient,
+    totals,
     offsets,
     weights,
-    estimate,
-    direction,
-    prev_mean,
-    new_estimate,
-    new_direction,
     raw,
     tmp,
     ext,
@@ -58,8 +60,7 @@
     own_in,
     grad,
     factors,
-    red_c,
-    red_x,
+    red_s,
     red_z,
     loc_sem,
     misc_sem,
@@ -76,10 +77,8 @@
     r_recv,
     o_send,
     o_recv,
-    rc_send,
-    rc_recv,
-    rx_send,
-    rx_recv,
+    rs_send,
+    rs_recv,
     rz_send,
     rz_recv,
 ):
@@ -104,6 +103,8 @@
     local = [
         pltpu.make_async_copy(estimate, est.at[pl.ds(0, here)], misc_sem.at[0]),
         pltpu.make_async_copy(direction, dirs.at[pl.ds(0, here)], misc_sem.at[1]),
+        pltpu.make_async_copy(offsets_in, offsets, misc_sem.at[2]),
+        pltpu.make_async_copy(weights_in, weights, misc_sem.at[3]),
     ]
 
     def tile_in(b):
@@ -113,16 +114,27 @@
 
     local[1].start()
     local[0].start()
+    local[2].start()
+    local[3].start()
     for b in range(here):
         tile_in(b).start()
 
     barrier = pltpu.get_barrier_semaphore()
-    for axis, size, me in (("epoch", nz, z), ("space", nx, x), ("sub", nc, c)):
-        for by in range(1, size):
-            pl.semaphore_signal(
-                barrier, inc=1, device_id={axis: lax.rem(me + by, size)}, device_id_type=MESH
-            )
-    pl.semaphore_wait(barrier, nz + nx + nc - 3)
+    spread = nx * nc
+    place = x * nc + c
+
+    def along_z(by):
+        return {"epoch": lax.rem(z + by, nz)}
+
+    def in_plane(by):
+        other = lax.rem(place + by, spread)
+        return {"space": other // nc, "sub": lax.rem(other, nc)}
+
+    for by in range(1, nz):
+        pl.semaphore_signal(barrier, inc=1, device_id=along_z(by), device_id_type=MESH)
+    for by in range(1, spread):
+        pl.semaphore_signal(barrier, inc=1, device_id=in_plane(by), device_id_type=MESH)
+    pl.semaphore_wait(barrier, nz + spread - 2)
 
     def remote(src, dst, send, recv, device):
         return pltpu.make_async_remote_copy(
@@ -204,13 +216,17 @@
 
     for k in range(OFFS):
         x_start(k, True)
-    for k in range(OFFS):
-        z_est(k).start()
-        z_tile(k).start()
+    for k in range(OFFS + LAG):
+        if k < OFFS:
+            z_tile(k).start()
+        if k >= LAG:
+            z_est(k - LAG).start()
     local[1].wait()
     dir_low[...] = dirs[pl.ds(0, OFFS)].astype(BF16)
     acc[...] = jnp.zeros_like(acc)
-    local[0].wait()
+    for copy in (local[0], local[2], local[3]):
+        copy.wait()
+    z_dir().start()
 
     row_at = lax.broadcasted_iota(jnp.int32, (ext_rows, LANES), 0)
     lane_at = lax.broadcasted_iota(jnp.int32, (ext_rows, LANES), 1)
@@ -298,7 +314,6 @@
             prepare(b - 1)
             pairs_of(b - 1)
 
-    z_dir().start()
     c_rim(here - 1).wait_recv()
     prepare(here - 1)
     pairs_of(here - 1)
@@ -325,12 +340,15 @@
     @pl.loop(OFFS, here)
     def _(k):
         grad[k] = acc[k]
+        gradient[k] = acc[k]
 
     @pl.loop(0, OFFS)
     def _(k):
         returned(k).wait_recv()
         owned(k).wait_recv()
-        grad[k] = acc[k] + ret_in[k]
+        whole = acc[k] + ret_in[k]
+        grad[k] = whole
+        gradient[k] = whole
         grad[here + k] = own_in[k].astype(F32) + acc[here + k]
 
     def one_epoch(e, sums):
@@ -357,10 +375,9 @@
         whole = jnp.sum(jnp.sum(value, axis=0, keepdims=True), axis=1, keepdims=True)
         tile = jnp.where(tile_row == index, whole, tile)
 
-    for axis, size, me, red, send, recv in (
-        ("sub", nc, c, red_c, rc_send, rc_recv),
-        ("space", nx, x, red_x, rx_send, rx_recv),
-        ("epoch", nz, z, red_z, rz_send, rz_recv),
+    for size, me, peer, red, send, recv in (
+        (spread, place, in_plane, red_s, rs_send, rs_recv),
+        (nz, z, along_z, red_z, rz_send, rz_recv),
     ):
         if size == 1:
             continue
@@ -368,11 +385,7 @@
 
         def share(by, source):
             return remote(
-                red.at[source],
-                red.at[source],
-                send.at[by],
-                recv.at[source],
-                {axis: lax.rem(me + by, size)},
+                red.at[source], red.at[source], send.at[by], recv.at[source], peer(by)
             )
 
         for by in range(1, size):
@@ -384,18 +397,7 @@
         tile = red[0]
         for source in range(1, size):
             tile = tile + red[source]
-
-    grad_norm, crossed, grad_term, mixed_term, old_term = (tile[i : i + 1, 0:1] for i in range(5))
-    cell_count = float(here * nz * look_rows * nx * cols * nc)
-    momentum = grad_norm / cell_count / prev_mean[0]
-    curvature = grad_term + 2.0 * momentum * mixed_term + momentum * momentum * old_term
-    step = (grad_norm + momentum * crossed) / curvature
-
-    @pl.loop(0, here)
-    def _(e):
-        moved = grad[e] + momentum * dirs[e]
-        new_direction[e] = moved
-        new_estimate[e] = est[e] + step * moved
+    totals[...] = tile
 
     @pl.loop(0, OFFS)
     def _(k):
@@ -430,6 +432,8 @@
     grid_cell = (look_rows, cols)
     dma = pltpu.SemaphoreType.DMA
     scratch = [
+        pltpu.SMEM(offsets.shape, jnp.int32),
+        pltpu.SMEM(weights.shape, F32),
         pltpu.VMEM((every, 2, total_rows, wide), BF16),
         pltpu.VMEM((2, wide // LANES, total_rows, LANES), F32),
         pltpu.VMEM((every, 2, LOOK, ext_rows, wide), F32),
@@ -444,11 +448,10 @@
         pltpu.VMEM((OFFS,) + grid_cell, BF16),
         pltpu.VMEM((every,) + grid_cell, F32),
         pltpu.VMEM((here * (OFFS + 1),) + grid_cell, F32),
-        pltpu.VMEM((nc, 8, LANES), F32),
-        pltpu.VMEM((nx, 8, LANES), F32),
+        pltpu.VMEM((nx * nc, 8, LANES), F32),
         pltpu.VMEM((nz, 8, LANES), F32),
         dma((here,)),
-        dma((2,)),
+        dma((4,)),
         dma((OFFS,)),
         dma((OFFS,)),
         dma((OFFS,)),
@@ -462,30 +465,34 @@
         dma((OFFS,)),
         dma((OFFS,)),
         dma((OFFS,)),
-        dma((nc,)),
-        dma((nc,)),
-        dma((nx,)),
-        dma((nx,)),
+        dma((nx * nc,)),
+        dma((nx * nc,)),
         dma((nz,)),
         dma((nz,)),
     ]
     anywhere = pl.BlockSpec(memory_space=pl.ANY)
-    scalars = pl.BlockSpec(memory_space=pltpu.SMEM)
     vectors = pl.BlockSpec(memory_space=pltpu.VMEM)
-    out = jax.ShapeDtypeStruct(estimate.shape, F32)
-    return tuple(
-        pl.pallas_call(
-            functools.partial(step_kernel, sizes),
-            name="cg_step",
-            out_shape=(out, out),
-            in_specs=[anywhere, scalars, scalars, anywhere, anywhere, scalars],
-            out_specs=(vectors, vectors),
-            scratch_shapes=scratch,
-            compiler_params=pltpu.CompilerParams(
-                collective_id=0, has_side_effects=True, vmem_limit_bytes=60 * 1024 * 1024
-            ),
-        )(slc, offsets, weights, estimate, direction, prev_mean)
-    )
+    gradient, totals = pl.pallas_call(
+        functools.partial(step_kernel, sizes),
+        name="cg_step",
+        out_shape=(
+            jax.ShapeDtypeStruct(estimate.shape, F32),
+            jax.ShapeDtypeStruct((8, LANES), F32),
+        ),
+        in_specs=[anywhere] * 5,
+        out_specs=(vectors, vectors),
+        scratch_shapes=scratch,
+        compiler_params=pltpu.CompilerParams(
+            collective_id=0, has_side_effects=True, vmem_limit_bytes=60 * 1024 * 1024
+        ),
+    )(slc, offsets, weights, estimate, direction)
+    grad_norm, crossed, grad_term, mixed_term, old_term = (totals[i, 0] for i in range(5))
+    cell_count = float(estimate.size * nz * nx * nc)
+    momentum = grad_norm / cell_count / prev_mean[0]
+    curvature = grad_term + 2.0 * momentum * mixed_term + momentum * momentum * old_term
+    step = (grad_norm + momentum * crossed) / curvature
+    moved = gradient + momentum * direction
+    return (estimate + step * moved, moved)
 
 
 def solution(mesh):

time: 68 us -> 70.1 us (1.031)
  between operations: 1.3 us -> 5.34 us
  Pallas kernels: 62 us -> 59.9 us
  other arithmetic: 0 us -> 1.81 us
  local copies, waits for them, and re-layouts: 4.45 us -> 2.84 us
    unnamed x8 -> x10, local copies, waits for them, and re-layouts: 4.45 us -> 1.37 us
    pallas_call x1, Pallas kernels: 62 us -> 59.9 us  [on_device(): pl.pallas_call(functools.partial(step_kernel, sizes), name='cg_step', out...]
    add x0 -> x1, other arithmetic: none -> 1.81 us  [on_device(): return (estimate + step * moved, moved)]
    slice x0 -> x1, local copies, waits for them, and re-layouts: none -> 1.47 us  [on_device(): totals[i, 0]]
where the time goes in v2:
time: 70.1 us; the launch traced here: 69.9 us
  Pallas kernels  59.9 us (85%)
  between operations  5.34 us (8%)
  local copies, waits for them, and re-layouts  2.84 us (4%)
  other arithmetic  1.81 us (3%)
    pallas_call x1, Pallas kernels, on_device(): pl.pallas_call(functools.partial(step_kernel, sizes), name='cg_step', out...  59.9 us
    add x1, other arithmetic, on_device(): return (estimate + step * moved, moved)  1.81 us
    slice x1, local copies, waits for them, and re-layouts, on_device(): totals[i, 0]  1.47 us

profile of v2, /device:TPU:0, one launch (start us, length us, event | category | flops | bytes accessed | tf_op | source)
XLA Modules:
  0.0 69.9 jit_solution(7345861532026749474)
XLA Ops:
  0.6 0.0 copy-start.2
  1.3 0.0 copy-done.2
  1.3 0.0 copy-start.3
  1.3 0.7 copy.8.offsets_in
  2.0 0.0 copy-done.3
  2.0 0.7 copy.9.weights_in
  2.7 0.0 copy-start
  2.7 0.0 copy-start.1
  2.7 59.9 %cg_step.1 = (f32[8,16,512]{2,1,0:T(8,128)}, f32[8,128]{1,0:T(8,128)}) custom-call(bf16[2,8,64,512]{3,2,1,0:T(8,128)(2,1)} %slc.1, s32[8,4]{1,0:T(8,128)} %copy.8.offsets_in, f32[8,4]{1,0:T(8,128)} %copy.9.weights_in, f32[8,16,512]{2,1,0:T(8,128)} %estimate.1, f32[8,16,512]{2,1,0:T(8,128)} %direction.1), custom_call_target="tpu_custom_call" | custom-call | tf_op jit(solution)/shard_map/cg_step/pallas_call | solution.py:475
  62.6 1.5 %fusion = (f32[1,1]{1,0:T(1,128)}, f32[1,1]{1,0:T(1,128)}, f32[1,1]{1,0:T(1,128)}, f32[1,1]{1,0:T(1,128)}, f32[1,1]{1,0:T(1,128)}) fusion(f32[8,128]{1,0:T(8,128)} %get-tuple-element.4), kind=kLoop, calls=%fused_computation.2 | loop fusion | bytes 40 | tf_op jit(solution)/shard_map/slice | solution.py:489
  68.0 0.0 copy-done
  68.0 0.0 copy-done.1
  68.0 1.8 %multiply_add_fusion = (f32[8,16,512]{2,1,0:T(8,128)}, f32[8,16,512]{2,1,0:T(8,128)}) fusion(f32[8,16,512]{2,1,0:T(8,128)S(1)} %copy-done, f32[]{:T(128)S(6)} %div.11, f32[8,16,512]{2,1,0:T(8,128)} %get-tuple-element.5, f32[8,16,512]{2,1,0:T(8,128)S(1)} %copy-done.1, f32[]{:T(128)S(6)} %div.10), kind=kLoop, calls=%fused_computation | loop fusion | flops 262144 | bytes 1310728 | tf_op jit(solution)/shard_map/add | solution.py:495
Async XLA Ops:
  0.6 0.7 copy-start.2
  1.3 0.7 copy-start.3
  2.7 65.4 %copy-start = (f32[8,16,512]{2,1,0:T(8,128)S(1)}, f32[8,16,512]{2,1,0:T(8,128)}, u32[]{:S(2)}) copy-start(f32[8,16,512]{2,1,0:T(8,128)} %estimate.1) | copy-start | bytes 786436
  2.7 65.4 %copy-start.1 = (f32[8,16,512]{2,1,0:T(8,128)S(1)}, f32[8,16,512]{2,1,0:T(8,128)}, u32[]{:S(2)}) copy-start(f32[8,16,512]{2,1,0:T(8,128)} %direction.1) | copy-start | bytes 786436

commit v3 on v2

--- a/solution.py
+++ b/solution.py
@@ -42,8 +42,10 @@
     weights_in,
     estimate,
     direction,
+    prev_mean,
     gradient,
-    totals,
+    momenta,
+    steps,
     offsets,
     weights,
     raw,
@@ -276,7 +278,7 @@
         weight = jnp.float32(0.0)
         for slot in range(SLOTS):
             weight = weight + jnp.where(
-                offsets[e, slot] == distance, weights[e, slot], jnp.float32(0.0)
+                offsets[slot, e] == distance, weights[slot, e], jnp.float32(0.0)
             )
         root = 1.0 / jnp.sqrt(pbox[e] * pbox[b] + EPSILON)
         real = real * root
@@ -358,7 +360,7 @@
         norm = norm + folded(g * g)
         crossed = crossed + folded(g * d)
         for slot in range(SLOTS):
-            far = offsets[e, slot]
+            far = offsets[slot, e]
             f = factors[e * (OFFS + 1) + far]
             dg = g - grad[e + far]
             ds = d - dirs[e + far]
@@ -397,7 +399,12 @@
         tile = red[0]
         for source in range(1, size):
             tile = tile + red[source]
-    totals[...] = tile
+    grad_norm, crossed, grad_term, mixed_term, old_term = (tile[i : i + 1, 0:1] for i in range(5))
+    cell_count = float(here * look_rows * cols * nz * nx * nc)
+    momentum = grad_norm / cell_count / prev_mean[0]
+    curvature = grad_term + 2.0 * momentum * mixed_term + momentum * momentum * old_term
+    momenta[...] = jnp.broadcast_to(momentum, momenta.shape)
+    steps[...] = jnp.broadcast_to((grad_norm + momentum * crossed) / curvature, steps.shape)
 
     @pl.loop(0, OFFS)
     def _(k):
@@ -432,8 +439,8 @@
     grid_cell = (look_rows, cols)
     dma = pltpu.SemaphoreType.DMA
     scratch = [
-        pltpu.SMEM(offsets.shape, jnp.int32),
-        pltpu.SMEM(weights.shape, F32),
+        pltpu.SMEM(offsets.shape[::-1], jnp.int32),
+        pltpu.SMEM(weights.shape[::-1], F32),
         pltpu.VMEM((every, 2, total_rows, wide), BF16),
         pltpu.VMEM((2, wide // LANES, total_rows, LANES), F32),
         pltpu.VMEM((every, 2, LOOK, ext_rows, wide), F32),
@@ -472,27 +479,23 @@
     ]
     anywhere = pl.BlockSpec(memory_space=pl.ANY)
     vectors = pl.BlockSpec(memory_space=pltpu.VMEM)
-    gradient, totals = pl.pallas_call(
+    gradient, momenta, steps = pl.pallas_call(
         functools.partial(step_kernel, sizes),
         name="cg_step",
         out_shape=(
             jax.ShapeDtypeStruct(estimate.shape, F32),
-            jax.ShapeDtypeStruct((8, LANES), F32),
+            jax.ShapeDtypeStruct((1,) + grid_cell, F32),
+            jax.ShapeDtypeStruct((1,) + grid_cell, F32),
         ),
-        in_specs=[anywhere] * 5,
-        out_specs=(vectors, vectors),
+        in_specs=[anywhere] * 5 + [pl.BlockSpec(memory_space=pltpu.SMEM)],
+        out_specs=(vectors, vectors, vectors),
         scratch_shapes=scratch,
         compiler_params=pltpu.CompilerParams(
             collective_id=0, has_side_effects=True, vmem_limit_bytes=60 * 1024 * 1024
         ),
-    )(slc, offsets, weights, estimate, direction)
-    grad_norm, crossed, grad_term, mixed_term, old_term = (totals[i, 0] for i in range(5))
-    cell_count = float(estimate.size * nz * nx * nc)
-    momentum = grad_norm / cell_count / prev_mean[0]
-    curvature = grad_term + 2.0 * momentum * mixed_term + momentum * momentum * old_term
-    step = (grad_norm + momentum * crossed) / curvature
-    moved = gradient + momentum * direction
-    return (estimate + step * moved, moved)
+    )(slc, offsets.T, weights.T, estimate, direction, prev_mean)
+    moved = gradient + momenta * direction
+    return (estimate + steps * moved, moved)
 
 
 def solution(mesh):

time: 70.1 us -> 63.3 us (0.903)
  between operations: 5.34 us -> 1.32 us
  local copies, waits for them, and re-layouts: 2.84 us -> 0.01 us
    slice x1 -> x0, local copies, waits for them, and re-layouts: 1.47 us -> none  [on_device(): totals[i, 0]]
    unnamed x10 -> x4, local copies, waits for them, and re-layouts: 1.37 us -> 0.01 us
where the time goes in v3:
time: 63.3 us; the launch traced here: 63.1 us
  Pallas kernels  60 us (95%)
  other arithmetic  1.82 us (3%)
  between operations  1.32 us (2%)
    pallas_call x1, Pallas kernels, on_device(): pl.pallas_call(functools.partial(step_kernel, sizes), name='cg_step', out...  60 us
    add x1, other arithmetic, on_device(): return (estimate + steps * moved, moved)  1.82 us

profile of v3, /device:TPU:0, one launch (start us, length us, event | category | flops | bytes accessed | tf_op | source)
XLA Modules:
  0.0 63.1 jit_solution(17425201454362317403)
XLA Ops:
  1.3 0.0 copy-start
  1.3 0.0 copy-start.1
  1.3 60.0 %cg_step.1 = (f32[8,16,512]{2,1,0:T(8,128)}, f32[1,16,512]{2,1,0:T(8,128)}, f32[1,16,512]{2,1,0:T(8,128)}) custom-call(bf16[2,8,64,512]{3,2,1,0:T(8,128)(2,1)} %slc.1, s32[4,8]{1,0:T(4,128)} %bitcast.6, f32[4,8]{1,0:T(4,128)} %bitcast.7, f32[8,16,512]{2,1,0:T(8,128)} %estimate.1, f32[8,16,512]{2,1,0:T(8,128)} %direction.1, f32[1]{0:T(128)S(6)} %copy.8.prev_mean), custom_call_target="tpu_custom_call" | custom-call | tf_op jit(solution)/shard_map/cg_step/pallas_call | solution.py:482
  61.3 0.0 copy-done
  61.3 0.0 copy-done.1
  61.3 1.8 %multiply_add_fusion = (f32[8,16,512]{2,1,0:T(8,128)}, f32[8,16,512]{2,1,0:T(8,128)}) fusion(f32[8,16,512]{2,1,0:T(8,128)S(1)} %copy-done, f32[16,512]{1,0:T(8,128)} %bitcast.5, f32[8,16,512]{2,1,0:T(8,128)} %get-tuple-element.6, f32[8,16,512]{2,1,0:T(8,128)S(1)} %copy-done.1, f32[16,512]{1,0:T(8,128)} %bitcast.4), kind=kLoop, calls=%fused_computation | loop fusion | flops 262144 | bytes 1376256 | tf_op jit(solution)/shard_map/add | solution.py:498
Async XLA Ops:
  1.3 60.0 %copy-start = (f32[8,16,512]{2,1,0:T(8,128)S(1)}, f32[8,16,512]{2,1,0:T(8,128)}, u32[]{:S(2)}) copy-start(f32[8,16,512]{2,1,0:T(8,128)} %estimate.1) | copy-start | bytes 786436
  1.3 60.0 %copy-start.1 = (f32[8,16,512]{2,1,0:T(8,128)S(1)}, f32[8,16,512]{2,1,0:T(8,128)}, u32[]{:S(2)}) copy-start(f32[8,16,512]{2,1,0:T(8,128)} %direction.1) | copy-start | bytes 786436
